TPU v7x, 512 devices: a whole 4x4x16 slice. The times are simulated.
512 devices in a mesh: depth: 8 (over x, core), strip: 64 (over y, z).
Axes of the slice: x: 4, y: 4, z: 16, core: 2. Of those that a mesh axis runs over, the one named last changes fastest.
Arguments:
- surface: float32 [2, 4, 1024, 1024], P(None, None, 'strip'), may hold values from -6 to 6
- velocity_class: int32 [8, 1024, 1024], P('depth', 'strip'), may hold values from 0 to 7
- table: float32 [2, 8, 2, 10], replicated, may hold values from -2 to 2
Outputs:
- image: float32 [8, 1024, 1024], P('depth', 'strip')
All inputs are finite; a program needn't handle non-finite values.
Results may differ from a plain program's by a relative error of at most 0.00017.
Values sent between devices are 32-bit elements; how exact they have to be, the bound alone decides.
No kernel may reach another device: no remote copies, remote signals or barrier semaphores. Data moves between devices by JAX's collectives and lax.ppermute only.
A program may use at most 64 MiB of HBM per device.

v0:
```python
import jax
import jax.numpy as jnp
from jax import lax
from jax.sharding import PartitionSpec as P

PASSES = 9
CLASSES = 8


def extended(shard, sides, width):
    for axis, dim in sides:
        devices, length = (lax.axis_size(axis), shard.shape[dim])
        up = [(i, (i + 1) % devices) for i in range(devices - 1)]
        down = [(j, i) for i, j in up]
        last = lax.slice_in_dim(shard, length - width, length, axis=dim)
        initial = lax.slice_in_dim(shard, 0, width, axis=dim)
        before = lax.ppermute(last, axis, up)
        after = lax.ppermute(initial, axis, down)
        shard = jnp.concatenate([before, shard, after], axis=dim)
    return shard


def mcclellan(field):
    lead = [(0, 0)] * (field.ndim - 2)
    padded = jnp.pad(field, lead + [(1, 1), (1, 1)])
    beside = (
        padded[..., 2:, 1:-1]
        + padded[..., :-2, 1:-1]
        + padded[..., 1:-1, 2:]
        + padded[..., 1:-1, :-2]
    )
    corners = (
        padded[..., 2:, 2:] + padded[..., 2:, :-2] + padded[..., :-2, 2:] + padded[..., :-2, :-2]
    )
    return -0.5 * field + 0.25 * beside + 0.125 * corners


def weigh(result, field, real_part, imag_part):
    return jnp.stack(
        [
            result[:, 0] + (real_part * field[:, 0] - imag_part * field[:, 1]),
            result[:, 1] + (real_part * field[:, 1] + imag_part * field[:, 0]),
            result[:, 2] + (real_part * field[:, 2] + imag_part * field[:, 3]),
            result[:, 3] + (real_part * field[:, 3] - imag_part * field[:, 2]),
        ],
        axis=1,
    )


def correlate(fields):
    total = jnp.zeros(fields.shape[2:], jnp.float32)
    for freq_index in range(fields.shape[0]):
        total = total + (
            fields[freq_index, 0] * fields[freq_index, 2]
            + fields[freq_index, 1] * fields[freq_index, 3]
        )
    return total


def tile_halo(sending, rim_width):
    return extended(sending, (("depth", 4), ("strip", 3)), rim_width)


def clip_domain(field, rim_width):
    row_count = field.shape[-2] - 2 * rim_width
    row_ids = (
        lax.axis_index("strip") * row_count
        - rim_width
        + jnp.arange(field.shape[-2], dtype=jnp.int32)
    )
    keep = ((row_ids >= 0) & (row_ids < row_count * lax.axis_size("strip")))[:, None]
    col_count = field.shape[-1] - 2 * rim_width
    col_ids = (
        lax.axis_index("depth") * col_count
        - rim_width
        + jnp.arange(field.shape[-1], dtype=jnp.int32)
    )
    keep = keep & ((col_ids >= 0) & (col_ids < col_count * lax.axis_size("depth")))[None, :]
    return jnp.where(keep, field, 0.0)


def chebyshev(fields, onehot, table_part, rim_width, widen):
    row_count = fields.shape[-2]
    col_count = fields.shape[-1]

    def own_cells(field):
        inner = field[..., rim_width : rim_width + row_count, :]
        inner = inner[..., rim_width : rim_width + col_count]
        return inner

    def coefficients(degree):
        pair = jnp.einsum(
            "cij,fcp->fpij", onehot, table_part[:, :, :, degree], precision=lax.Precision.HIGHEST
        )
        return (pair[:, 0], pair[:, 1])

    real_part, imag_part = coefficients(0)
    result = weigh(jnp.zeros_like(fields), fields, real_part, imag_part)
    previous = fields
    current = fields
    for block_index in range(PASSES // rim_width):
        sending = current[None] if block_index == 0 else jnp.stack([previous, current])
        widened = widen(sending, rim_width)
        wide_prev = widened[0]
        wide_curr = widened[-1]
        for inner_pass in range(rim_width):
            degree = block_index * rim_width + inner_pass
            if degree == 0:
                following = mcclellan(wide_curr)
            else:
                following = 2.0 * mcclellan(wide_curr) - wide_prev
            following = clip_domain(following, rim_width)
            wide_prev, wide_curr = (wide_curr, following)
            real_part, imag_part = coefficients(degree + 1)
            result = weigh(result, own_cells(wide_curr), real_part, imag_part)
        previous = own_cells(wide_prev)
        current = own_cells(wide_curr)
    return result


def body(surface, velocity_class, table):
    classes = jnp.arange(CLASSES, dtype=jnp.int32)
    rim_width = 3
    velocity = lax.all_to_all(velocity_class, "depth", split_axis=2, concat_axis=0, tiled=True)
    col_count = velocity.shape[2]
    fields = lax.dynamic_slice_in_dim(surface, lax.axis_index("depth") * col_count, col_count, 3)

    def descend(level_index, state_pair):
        level_fields, image = state_pair
        classes_here = lax.dynamic_index_in_dim(velocity, level_index, 0, keepdims=False)
        onehot = (classes_here[None] == classes[:, None, None]).astype(jnp.float32)
        level_fields = chebyshev(level_fields, onehot, table, rim_width, tile_halo)
        image = lax.dynamic_update_index_in_dim(image, correlate(level_fields), level_index, 0)
        return (level_fields, image)

    initial = (fields, jnp.zeros((velocity.shape[0], velocity.shape[1], col_count), jnp.float32))
    fields, image = lax.fori_loop(0, velocity.shape[0], descend, initial)
    return lax.all_to_all(image, "depth", split_axis=0, concat_axis=2, tiled=True)


def solution(mesh):
    in_specs = (P(None, None, "strip", None), P("depth", "strip", None), P())
    out_specs = P("depth", "strip", None)
    return jax.shard_map(body, mesh=mesh, in_specs=in_specs, out_specs=out_specs, check_vma=False)
```

profile of v0, /device:TPU:24, one launch (start us, length us, event | category | flops | bytes accessed | tf_op | source)
XLA Modules:
  0.0 554.1 jit_solution(4502682108848891029)
XLA Ops:
  4.6 4.3 all-to-all-start
  9.7 4.8 all-to-all-done
  16.5 522.7 %while.19 = (s32[]{:T(128)}, f32[2,4,16,128]{3,1,0,2:T(4,128)S(1)}, f32[8,16,128]{2,1,0:T(8,128)S(1)}, s32[8,16,128]{2,0,1:T(8,128)S(1)}, f32[2,8,2,10]{1,2,0,3:...) while((s32[]{:T(128)}, f32[2,4,16,128]{3,1,0,2:T(4,128)S(1)}, ...), condition=%wide.region_1.2_spmd.clone, body=%wide.region_0.1_spmd.clone.sunk | while | flops 12695103 | bytes 9011121 | solution.py:137
  22.6 11.6 %collective-permute-start.2 = (f32[1,2,4,3,134]{4,2,1,3,0:T(4,128)S(1)}, f32[1,2,4,3,134]{4,2,1,3,0:T(4,128)S(1)}, u32[]{:S(2)}, u32[]{:S(2)}) collective-permute-start(f32[1,2,4,3,134]{4,2,1,3,0:T(4,128)S(1)} %get-tuple-element.279), channel_id=1, source_target_pairs={{1,0},{2,1},{3,2},{4,3},{5,4},{6,5},{7,6},{8,7},{9,8},{10,9},{11,1... | collective-permute-start | bytes 38600 | tf_op jit(solution)/shard_map/while/body/eval_jaxpr/ppermute | solution.py:18
  36.2 5.8 %collective-permute-done.3 = f32[1,2,4,3,134]{4,2,1,3,0:T(4,128)S(1)} collective-permute-done((f32[1,2,4,3,134]{4,2,1,3,0:T(4,128)S(1)}, f32[1,2,4,3,134]{4,2,1,3,0:T(4,128)S(1)}, u32[]{:S(2)}, u32[]{:S(2)}) %collective-permute-start.3) | collective-permute-done | bytes 12896 | tf_op jit(solution)/shard_map/while/body/eval_jaxpr/ppermute | solution.py:17
  64.2 5.2 collective-permute-start.9
  87.1 5.9 %collective-permute-start.1 = (f32[1,2,4,16,3]{4,2,1,3,0:T(4,128)S(1)}, f32[1,2,4,16,3]{4,2,1,3,0:T(4,128)S(1)}, u32[]{:S(2)}, u32[]{:S(2)}) collective-permute-start(f32[1,2,4,16,3]{4,2,1,3,0:T(4,128)S(1)} %get-tuple-element.278), channel_id=1, source_target_pairs={{0,64},{64,128},{128,192},{192,256},{256,320},{320,384},{384,448},... | collective-permute-start | bytes 4616 | tf_op jit(solution)/shard_map/while/body/eval_jaxpr/ppermute | solution.py:17
  108.4 5.0 collective-permute-start.5
  128.3 5.9 %collective-permute-start.9 = (f32[2,2,4,16,3]{4,2,1,3,0:T(4,128)S(1)}, f32[2,2,4,16,3]{4,2,1,3,0:T(4,128)S(1)}, u32[]{:S(2)}, u32[]{:S(2)}) collective-permute-start(f32[2,2,4,16,3]{4,2,1,3,0:T(4,128)S(1)} %get-tuple-element.288), channel_id=1, source_target_pairs={{0,64},{64,128},{128,192},{192,256},{256,320},{320,384},{384,448},... | collective-permute-start | bytes 9224 | tf_op jit(solution)/shard_map/while/body/eval_jaxpr/ppermute | solution.py:17
  151.9 5.9 %collective-permute-start.1 = (f32[1,2,4,16,3]{4,2,1,3,0:T(4,128)S(1)}, f32[1,2,4,16,3]{4,2,1,3,0:T(4,128)S(1)}, u32[]{:S(2)}, u32[]{:S(2)}) collective-permute-start(f32[1,2,4,16,3]{4,2,1,3,0:T(4,128)S(1)} %get-tuple-element.278), channel_id=1, source_target_pairs={{0,64},{64,128},{128,192},{192,256},{256,320},{320,384},{384,448},... | collective-permute-start | bytes 4616 | tf_op jit(solution)/shard_map/while/body/eval_jaxpr/ppermute | solution.py:17
  173.2 5.0 collective-permute-start.5
  185.4 4.0 collective-permute-done.7
  193.1 5.9 %collective-permute-start.9 = (f32[2,2,4,16,3]{4,2,1,3,0:T(4,128)S(1)}, f32[2,2,4,16,3]{4,2,1,3,0:T(4,128)S(1)}, u32[]{:S(2)}, u32[]{:S(2)}) collective-permute-start(f32[2,2,4,16,3]{4,2,1,3,0:T(4,128)S(1)} %get-tuple-element.288), channel_id=1, source_target_pairs={{0,64},{64,128},{128,192},{192,256},{256,320},{320,384},{384,448},... | collective-permute-start | bytes 9224 | tf_op jit(solution)/shard_map/while/body/eval_jaxpr/ppermute | solution.py:17
  216.7 5.9 %collective-permute-start.1 = (f32[1,2,4,16,3]{4,2,1,3,0:T(4,128)S(1)}, f32[1,2,4,16,3]{4,2,1,3,0:T(4,128)S(1)}, u32[]{:S(2)}, u32[]{:S(2)}) collective-permute-start(f32[1,2,4,16,3]{4,2,1,3,0:T(4,128)S(1)} %get-tuple-element.278), channel_id=1, source_target_pairs={{0,64},{64,128},{128,192},{192,256},{256,320},{320,384},{384,448},... | collective-permute-start | bytes 4616 | tf_op jit(solution)/shard_map/while/body/eval_jaxpr/ppermute | solution.py:17
  238.0 5.0 collective-permute-start.5
  250.2 4.0 collective-permute-done.7
  257.9 5.9 %collective-permute-start.9 = (f32[2,2,4,16,3]{4,2,1,3,0:T(4,128)S(1)}, f32[2,2,4,16,3]{4,2,1,3,0:T(4,128)S(1)}, u32[]{:S(2)}, u32[]{:S(2)}) collective-permute-start(f32[2,2,4,16,3]{4,2,1,3,0:T(4,128)S(1)} %get-tuple-element.288), channel_id=1, source_target_pairs={{0,64},{64,128},{128,192},{192,256},{256,320},{320,384},{384,448},... | collective-permute-start | bytes 9224 | tf_op jit(solution)/shard_map/while/body/eval_jaxpr/ppermute | solution.py:17
  281.5 5.9 %collective-permute-start.1 = (f32[1,2,4,16,3]{4,2,1,3,0:T(4,128)S(1)}, f32[1,2,4,16,3]{4,2,1,3,0:T(4,128)S(1)}, u32[]{:S(2)}, u32[]{:S(2)}) collective-permute-start(f32[1,2,4,16,3]{4,2,1,3,0:T(4,128)S(1)} %get-tuple-element.278), channel_id=1, source_target_pairs={{0,64},{64,128},{128,192},{192,256},{256,320},{320,384},{384,448},... | collective-permute-start | bytes 4616 | tf_op jit(solution)/shard_map/while/body/eval_jaxpr/ppermute | solution.py:17
  302.8 5.0 collective-permute-start.5
  322.7 5.9 %collective-permute-start.9 = (f32[2,2,4,16,3]{4,2,1,3,0:T(4,128)S(1)}, f32[2,2,4,16,3]{4,2,1,3,0:T(4,128)S(1)}, u32[]{:S(2)}, u32[]{:S(2)}) collective-permute-start(f32[2,2,4,16,3]{4,2,1,3,0:T(4,128)S(1)} %get-tuple-element.288), channel_id=1, source_target_pairs={{0,64},{64,128},{128,192},{192,256},{256,320},{320,384},{384,448},... | collective-permute-start | bytes 9224 | tf_op jit(solution)/shard_map/while/body/eval_jaxpr/ppermute | solution.py:17
  346.3 5.9 %collective-permute-start.1 = (f32[1,2,4,16,3]{4,2,1,3,0:T(4,128)S(1)}, f32[1,2,4,16,3]{4,2,1,3,0:T(4,128)S(1)}, u32[]{:S(2)}, u32[]{:S(2)}) collective-permute-start(f32[1,2,4,16,3]{4,2,1,3,0:T(4,128)S(1)} %get-tuple-element.278), channel_id=1, source_target_pairs={{0,64},{64,128},{128,192},{192,256},{256,320},{320,384},{384,448},... | collective-permute-start | bytes 4616 | tf_op jit(solution)/shard_map/while/body/eval_jaxpr/ppermute | solution.py:17
  367.6 5.0 collective-permute-start.5
  379.8 4.0 collective-permute-done.7
  387.5 5.9 %collective-permute-start.9 = (f32[2,2,4,16,3]{4,2,1,3,0:T(4,128)S(1)}, f32[2,2,4,16,3]{4,2,1,3,0:T(4,128)S(1)}, u32[]{:S(2)}, u32[]{:S(2)}) collective-permute-start(f32[2,2,4,16,3]{4,2,1,3,0:T(4,128)S(1)} %get-tuple-element.288), channel_id=1, source_target_pairs={{0,64},{64,128},{128,192},{192,256},{256,320},{320,384},{384,448},... | collective-permute-start | bytes 9224 | tf_op jit(solution)/shard_map/while/body/eval_jaxpr/ppermute | solution.py:17
  411.0 5.9 %collective-permute-start.1 = (f32[1,2,4,16,3]{4,2,1,3,0:T(4,128)S(1)}, f32[1,2,4,16,3]{4,2,1,3,0:T(4,128)S(1)}, u32[]{:S(2)}, u32[]{:S(2)}) collective-permute-start(f32[1,2,4,16,3]{4,2,1,3,0:T(4,128)S(1)} %get-tuple-element.278), channel_id=1, source_target_pairs={{0,64},{64,128},{128,192},{192,256},{256,320},{320,384},{384,448},... | collective-permute-start | bytes 4616 | tf_op jit(solution)/shard_map/while/body/eval_jaxpr/ppermute | solution.py:17
  432.4 5.0 collective-permute-start.5
  444.6 4.0 collective-permute-done.7
  452.3 5.9 %collective-permute-start.9 = (f32[2,2,4,16,3]{4,2,1,3,0:T(4,128)S(1)}, f32[2,2,4,16,3]{4,2,1,3,0:T(4,128)S(1)}, u32[]{:S(2)}, u32[]{:S(2)}) collective-permute-start(f32[2,2,4,16,3]{4,2,1,3,0:T(4,128)S(1)} %get-tuple-element.288), channel_id=1, source_target_pairs={{0,64},{64,128},{128,192},{192,256},{256,320},{320,384},{384,448},... | collective-permute-start | bytes 9224 | tf_op jit(solution)/shard_map/while/body/eval_jaxpr/ppermute | solution.py:17
  475.8 5.9 %collective-permute-start.1 = (f32[1,2,4,16,3]{4,2,1,3,0:T(4,128)S(1)}, f32[1,2,4,16,3]{4,2,1,3,0:T(4,128)S(1)}, u32[]{:S(2)}, u32[]{:S(2)}) collective-permute-start(f32[1,2,4,16,3]{4,2,1,3,0:T(4,128)S(1)} %get-tuple-element.278), channel_id=1, source_target_pairs={{0,64},{64,128},{128,192},{192,256},{256,320},{320,384},{384,448},... | collective-permute-start | bytes 4616 | tf_op jit(solution)/shard_map/while/body/eval_jaxpr/ppermute | solution.py:17
  497.2 5.0 collective-permute-start.5
  517.1 5.9 %collective-permute-start.9 = (f32[2,2,4,16,3]{4,2,1,3,0:T(4,128)S(1)}, f32[2,2,4,16,3]{4,2,1,3,0:T(4,128)S(1)}, u32[]{:S(2)}, u32[]{:S(2)}) collective-permute-start(f32[2,2,4,16,3]{4,2,1,3,0:T(4,128)S(1)} %get-tuple-element.288), channel_id=1, source_target_pairs={{0,64},{64,128},{128,192},{192,256},{256,320},{320,384},{384,448},... | collective-permute-start | bytes 9224 | tf_op jit(solution)/shard_map/while/body/eval_jaxpr/ppermute | solution.py:17
  539.2 14.2 %all_to_all.36 = f32[8,16,128]{2,1,0:T(8,128)S(1)} all-to-all(f32[8,16,128]{2,1,0:T(8,128)S(1)} %get-tuple-element.180), channel_id=1, replica_groups=mesh['depth'=8,'strip'=64] {'depth'}, dimensions={0} | all-to-all | bytes 131072 | tf_op jit(solution)/shard_map/all_to_all | solution.py:138
  (532 shorter events, 370.7 us)
Async XLA Ops:
  4.6 9.9 %all-to-all-start = ((s32[8,1,2048]{2,1,0:T(1,128)}), s32[8,1,2048]{2,1,0:T(1,128)S(1)}, u32[]{:S(2)}, u32[]{:S(2)}) async-start(s32[8,1,2048]{2,1,0:T(1,128)} %reshape.214), calls=%async_computation | async-start | bytes 131072 | tf_op jit(solution)/shard_map/all_to_all | solution.py:124
  22.6 13.6 %collective-permute-start.2 = (f32[1,2,4,3,134]{4,2,1,3,0:T(4,128)S(1)}, f32[1,2,4,3,134]{4,2,1,3,0:T(4,128)S(1)}, u32[]{:S(2)}, u32[]{:S(2)}) collective-permute-start(f32[1,2,4,3,134]{4,2,1,3,0:T(4,128)S(1)} %get-tuple-element.279), channel_id=1, source_target_pairs={{1,0},{2,1},{3,2},{4,3},{5,4},{6,5},{7,6},{8,7},{9,8},{10,9},{11,1... | collective-permute-start | bytes 38600 | tf_op jit(solution)/shard_map/while/body/eval_jaxpr/ppermute | solution.py:18
  34.2 7.8 %collective-permute-start.3 = (f32[1,2,4,3,134]{4,2,1,3,0:T(4,128)S(1)}, f32[1,2,4,3,134]{4,2,1,3,0:T(4,128)S(1)}, u32[]{:S(2)}, u32[]{:S(2)}) collective-permute-start(f32[1,2,4,3,134]{4,2,1,3,0:T(4,128)S(1)} %get-tuple-element.280), channel_id=1, source_target_pairs={{0,1},{1,2},{2,3},{3,4},{4,5},{5,6},{6,7},{7,8},{8,9},{9,10},{10,1... | collective-permute-start | bytes 38600 | tf_op jit(solution)/shard_map/while/body/eval_jaxpr/ppermute | solution.py:17
  52.3 8.1 %collective-permute-start.7 = (f32[2,2,4,3,134]{4,2,1,3,0:T(4,128)S(1)}, f32[2,2,4,3,134]{4,2,1,3,0:T(4,128)S(1)}, u32[]{:S(2)}, u32[]{:S(2)}) collective-permute-start(f32[2,2,4,3,134]{4,2,1,3,0:T(4,128)S(1)} %get-tuple-element.286), channel_id=1, source_target_pairs={{0,1},{1,2},{2,3},{3,4},{4,5},{5,6},{6,7},{7,8},{8,9},{9,10},{10,1... | collective-permute-start | bytes 77192 | tf_op jit(solution)/shard_map/while/body/eval_jaxpr/ppermute | solution.py:17
  72.4 8.1 %collective-permute-start.11 = (f32[2,2,4,3,134]{4,2,1,3,0:T(4,128)S(1)}, f32[2,2,4,3,134]{4,2,1,3,0:T(4,128)S(1)}, u32[]{:S(2)}, u32[]{:S(2)}) collective-permute-start(f32[2,2,4,3,134]{4,2,1,3,0:T(4,128)S(1)} %get-tuple-element.290), channel_id=1, source_target_pairs={{0,1},{1,2},{2,3},{3,4},{4,5},{5,6},{6,7},{7,8},{8,9},{9,10},{10,1... | collective-permute-start | bytes 77192 | tf_op jit(solution)/shard_map/while/body/eval_jaxpr/ppermute | solution.py:17
  85.8 8.5 %collective-permute-start = (f32[1,2,4,16,3]{4,2,1,3,0:T(4,128)S(1)}, f32[1,2,4,16,3]{4,2,1,3,0:T(4,128)S(1)}, u32[]{:S(2)}, u32[]{:S(2)}) collective-permute-start(f32[1,2,4,16,3]{4,2,1,3,0:T(4,128)S(1)} %get-tuple-element.277), channel_id=1, source_target_pairs={{64,0},{128,64},{192,128},{256,192},{320,256},{384,320},{448,384},... | collective-permute-start | bytes 4616 | tf_op jit(solution)/shard_map/while/body/eval_jaxpr/ppermute | solution.py:18
  96.3 7.8 %collective-permute-start.3 = (f32[1,2,4,3,134]{4,2,1,3,0:T(4,128)S(1)}, f32[1,2,4,3,134]{4,2,1,3,0:T(4,128)S(1)}, u32[]{:S(2)}, u32[]{:S(2)}) collective-permute-start(f32[1,2,4,3,134]{4,2,1,3,0:T(4,128)S(1)} %get-tuple-element.280), channel_id=1, source_target_pairs={{0,1},{1,2},{2,3},{3,4},{4,5},{5,6},{6,7},{7,8},{8,9},{9,10},{10,1... | collective-permute-start | bytes 38600 | tf_op jit(solution)/shard_map/while/body/eval_jaxpr/ppermute | solution.py:17
  116.5 8.1 %collective-permute-start.7 = (f32[2,2,4,3,134]{4,2,1,3,0:T(4,128)S(1)}, f32[2,2,4,3,134]{4,2,1,3,0:T(4,128)S(1)}, u32[]{:S(2)}, u32[]{:S(2)}) collective-permute-start(f32[2,2,4,3,134]{4,2,1,3,0:T(4,128)S(1)} %get-tuple-element.286), channel_id=1, source_target_pairs={{0,1},{1,2},{2,3},{3,4},{4,5},{5,6},{6,7},{7,8},{8,9},{9,10},{10,1... | collective-permute-start | bytes 77192 | tf_op jit(solution)/shard_map/while/body/eval_jaxpr/ppermute | solution.py:17
  137.2 8.1 %collective-permute-start.11 = (f32[2,2,4,3,134]{4,2,1,3,0:T(4,128)S(1)}, f32[2,2,4,3,134]{4,2,1,3,0:T(4,128)S(1)}, u32[]{:S(2)}, u32[]{:S(2)}) collective-permute-start(f32[2,2,4,3,134]{4,2,1,3,0:T(4,128)S(1)} %get-tuple-element.290), channel_id=1, source_target_pairs={{0,1},{1,2},{2,3},{3,4},{4,5},{5,6},{6,7},{7,8},{8,9},{9,10},{10,1... | collective-permute-start | bytes 77192 | tf_op jit(solution)/shard_map/while/body/eval_jaxpr/ppermute | solution.py:17
  150.6 8.5 %collective-permute-start = (f32[1,2,4,16,3]{4,2,1,3,0:T(4,128)S(1)}, f32[1,2,4,16,3]{4,2,1,3,0:T(4,128)S(1)}, u32[]{:S(2)}, u32[]{:S(2)}) collective-permute-start(f32[1,2,4,16,3]{4,2,1,3,0:T(4,128)S(1)} %get-tuple-element.277), channel_id=1, source_target_pairs={{64,0},{128,64},{192,128},{256,192},{320,256},{384,320},{448,384},... | collective-permute-start | bytes 4616 | tf_op jit(solution)/shard_map/while/body/eval_jaxpr/ppermute | solution.py:18
  161.1 7.8 %collective-permute-start.3 = (f32[1,2,4,3,134]{4,2,1,3,0:T(4,128)S(1)}, f32[1,2,4,3,134]{4,2,1,3,0:T(4,128)S(1)}, u32[]{:S(2)}, u32[]{:S(2)}) collective-permute-start(f32[1,2,4,3,134]{4,2,1,3,0:T(4,128)S(1)} %get-tuple-element.280), channel_id=1, source_target_pairs={{0,1},{1,2},{2,3},{3,4},{4,5},{5,6},{6,7},{7,8},{8,9},{9,10},{10,1... | collective-permute-start | bytes 38600 | tf_op jit(solution)/shard_map/while/body/eval_jaxpr/ppermute | solution.py:17
  181.3 8.1 %collective-permute-start.7 = (f32[2,2,4,3,134]{4,2,1,3,0:T(4,128)S(1)}, f32[2,2,4,3,134]{4,2,1,3,0:T(4,128)S(1)}, u32[]{:S(2)}, u32[]{:S(2)}) collective-permute-start(f32[2,2,4,3,134]{4,2,1,3,0:T(4,128)S(1)} %get-tuple-element.286), channel_id=1, source_target_pairs={{0,1},{1,2},{2,3},{3,4},{4,5},{5,6},{6,7},{7,8},{8,9},{9,10},{10,1... | collective-permute-start | bytes 77192 | tf_op jit(solution)/shard_map/while/body/eval_jaxpr/ppermute | solution.py:17
  202.0 8.1 %collective-permute-start.11 = (f32[2,2,4,3,134]{4,2,1,3,0:T(4,128)S(1)}, f32[2,2,4,3,134]{4,2,1,3,0:T(4,128)S(1)}, u32[]{:S(2)}, u32[]{:S(2)}) collective-permute-start(f32[2,2,4,3,134]{4,2,1,3,0:T(4,128)S(1)} %get-tuple-element.290), channel_id=1, source_target_pairs={{0,1},{1,2},{2,3},{3,4},{4,5},{5,6},{6,7},{7,8},{8,9},{9,10},{10,1... | collective-permute-start | bytes 77192 | tf_op jit(solution)/shard_map/while/body/eval_jaxpr/ppermute | solution.py:17
  215.4 8.5 %collective-permute-start = (f32[1,2,4,16,3]{4,2,1,3,0:T(4,128)S(1)}, f32[1,2,4,16,3]{4,2,1,3,0:T(4,128)S(1)}, u32[]{:S(2)}, u32[]{:S(2)}) collective-permute-start(f32[1,2,4,16,3]{4,2,1,3,0:T(4,128)S(1)} %get-tuple-element.277), channel_id=1, source_target_pairs={{64,0},{128,64},{192,128},{256,192},{320,256},{384,320},{448,384},... | collective-permute-start | bytes 4616 | tf_op jit(solution)/shard_map/while/body/eval_jaxpr/ppermute | solution.py:18
  225.9 7.8 %collective-permute-start.3 = (f32[1,2,4,3,134]{4,2,1,3,0:T(4,128)S(1)}, f32[1,2,4,3,134]{4,2,1,3,0:T(4,128)S(1)}, u32[]{:S(2)}, u32[]{:S(2)}) collective-permute-start(f32[1,2,4,3,134]{4,2,1,3,0:T(4,128)S(1)} %get-tuple-element.280), channel_id=1, source_target_pairs={{0,1},{1,2},{2,3},{3,4},{4,5},{5,6},{6,7},{7,8},{8,9},{9,10},{10,1... | collective-permute-start | bytes 38600 | tf_op jit(solution)/shard_map/while/body/eval_jaxpr/ppermute | solution.py:17
  246.1 8.1 %collective-permute-start.7 = (f32[2,2,4,3,134]{4,2,1,3,0:T(4,128)S(1)}, f32[2,2,4,3,134]{4,2,1,3,0:T(4,128)S(1)}, u32[]{:S(2)}, u32[]{:S(2)}) collective-permute-start(f32[2,2,4,3,134]{4,2,1,3,0:T(4,128)S(1)} %get-tuple-element.286), channel_id=1, source_target_pairs={{0,1},{1,2},{2,3},{3,4},{4,5},{5,6},{6,7},{7,8},{8,9},{9,10},{10,1... | collective-permute-start | bytes 77192 | tf_op jit(solution)/shard_map/while/body/eval_jaxpr/ppermute | solution.py:17
  266.8 8.1 %collective-permute-start.11 = (f32[2,2,4,3,134]{4,2,1,3,0:T(4,128)S(1)}, f32[2,2,4,3,134]{4,2,1,3,0:T(4,128)S(1)}, u32[]{:S(2)}, u32[]{:S(2)}) collective-permute-start(f32[2,2,4,3,134]{4,2,1,3,0:T(4,128)S(1)} %get-tuple-element.290), channel_id=1, source_target_pairs={{0,1},{1,2},{2,3},{3,4},{4,5},{5,6},{6,7},{7,8},{8,9},{9,10},{10,1... | collective-permute-start | bytes 77192 | tf_op jit(solution)/shard_map/while/body/eval_jaxpr/ppermute | solution.py:17
  280.2 8.5 %collective-permute-start = (f32[1,2,4,16,3]{4,2,1,3,0:T(4,128)S(1)}, f32[1,2,4,16,3]{4,2,1,3,0:T(4,128)S(1)}, u32[]{:S(2)}, u32[]{:S(2)}) collective-permute-start(f32[1,2,4,16,3]{4,2,1,3,0:T(4,128)S(1)} %get-tuple-element.277), channel_id=1, source_target_pairs={{64,0},{128,64},{192,128},{256,192},{320,256},{384,320},{448,384},... | collective-permute-start | bytes 4616 | tf_op jit(solution)/shard_map/while/body/eval_jaxpr/ppermute | solution.py:18
  290.7 7.8 %collective-permute-start.3 = (f32[1,2,4,3,134]{4,2,1,3,0:T(4,128)S(1)}, f32[1,2,4,3,134]{4,2,1,3,0:T(4,128)S(1)}, u32[]{:S(2)}, u32[]{:S(2)}) collective-permute-start(f32[1,2,4,3,134]{4,2,1,3,0:T(4,128)S(1)} %get-tuple-element.280), channel_id=1, source_target_pairs={{0,1},{1,2},{2,3},{3,4},{4,5},{5,6},{6,7},{7,8},{8,9},{9,10},{10,1... | collective-permute-start | bytes 38600 | tf_op jit(solution)/shard_map/while/body/eval_jaxpr/ppermute | solution.py:17
  310.9 8.1 %collective-permute-start.7 = (f32[2,2,4,3,134]{4,2,1,3,0:T(4,128)S(1)}, f32[2,2,4,3,134]{4,2,1,3,0:T(4,128)S(1)}, u32[]{:S(2)}, u32[]{:S(2)}) collective-permute-start(f32[2,2,4,3,134]{4,2,1,3,0:T(4,128)S(1)} %get-tuple-element.286), channel_id=1, source_target_pairs={{0,1},{1,2},{2,3},{3,4},{4,5},{5,6},{6,7},{7,8},{8,9},{9,10},{10,1... | collective-permute-start | bytes 77192 | tf_op jit(solution)/shard_map/while/body/eval_jaxpr/ppermute | solution.py:17
  331.6 8.1 %collective-permute-start.11 = (f32[2,2,4,3,134]{4,2,1,3,0:T(4,128)S(1)}, f32[2,2,4,3,134]{4,2,1,3,0:T(4,128)S(1)}, u32[]{:S(2)}, u32[]{:S(2)}) collective-permute-start(f32[2,2,4,3,134]{4,2,1,3,0:T(4,128)S(1)} %get-tuple-element.290), channel_id=1, source_target_pairs={{0,1},{1,2},{2,3},{3,4},{4,5},{5,6},{6,7},{7,8},{8,9},{9,10},{10,1... | collective-permute-start | bytes 77192 | tf_op jit(solution)/shard_map/while/body/eval_jaxpr/ppermute | solution.py:17
  345.0 8.5 %collective-permute-start = (f32[1,2,4,16,3]{4,2,1,3,0:T(4,128)S(1)}, f32[1,2,4,16,3]{4,2,1,3,0:T(4,128)S(1)}, u32[]{:S(2)}, u32[]{:S(2)}) collective-permute-start(f32[1,2,4,16,3]{4,2,1,3,0:T(4,128)S(1)} %get-tuple-element.277), channel_id=1, source_target_pairs={{64,0},{128,64},{192,128},{256,192},{320,256},{384,320},{448,384},... | collective-permute-start | bytes 4616 | tf_op jit(solution)/shard_map/while/body/eval_jaxpr/ppermute | solution.py:18
  355.5 7.8 %collective-permute-start.3 = (f32[1,2,4,3,134]{4,2,1,3,0:T(4,128)S(1)}, f32[1,2,4,3,134]{4,2,1,3,0:T(4,128)S(1)}, u32[]{:S(2)}, u32[]{:S(2)}) collective-permute-start(f32[1,2,4,3,134]{4,2,1,3,0:T(4,128)S(1)} %get-tuple-element.280), channel_id=1, source_target_pairs={{0,1},{1,2},{2,3},{3,4},{4,5},{5,6},{6,7},{7,8},{8,9},{9,10},{10,1... | collective-permute-start | bytes 38600 | tf_op jit(solution)/shard_map/while/body/eval_jaxpr/ppermute | solution.py:17
  375.6 8.1 %collective-permute-start.7 = (f32[2,2,4,3,134]{4,2,1,3,0:T(4,128)S(1)}, f32[2,2,4,3,134]{4,2,1,3,0:T(4,128)S(1)}, u32[]{:S(2)}, u32[]{:S(2)}) collective-permute-start(f32[2,2,4,3,134]{4,2,1,3,0:T(4,128)S(1)} %get-tuple-element.286), channel_id=1, source_target_pairs={{0,1},{1,2},{2,3},{3,4},{4,5},{5,6},{6,7},{7,8},{8,9},{9,10},{10,1... | collective-permute-start | bytes 77192 | tf_op jit(solution)/shard_map/while/body/eval_jaxpr/ppermute | solution.py:17
  396.4 8.1 %collective-permute-start.11 = (f32[2,2,4,3,134]{4,2,1,3,0:T(4,128)S(1)}, f32[2,2,4,3,134]{4,2,1,3,0:T(4,128)S(1)}, u32[]{:S(2)}, u32[]{:S(2)}) collective-permute-start(f32[2,2,4,3,134]{4,2,1,3,0:T(4,128)S(1)} %get-tuple-element.290), channel_id=1, source_target_pairs={{0,1},{1,2},{2,3},{3,4},{4,5},{5,6},{6,7},{7,8},{8,9},{9,10},{10,1... | collective-permute-start | bytes 77192 | tf_op jit(solution)/shard_map/while/body/eval_jaxpr/ppermute | solution.py:17
  409.7 8.5 %collective-permute-start = (f32[1,2,4,16,3]{4,2,1,3,0:T(4,128)S(1)}, f32[1,2,4,16,3]{4,2,1,3,0:T(4,128)S(1)}, u32[]{:S(2)}, u32[]{:S(2)}) collective-permute-start(f32[1,2,4,16,3]{4,2,1,3,0:T(4,128)S(1)} %get-tuple-element.277), channel_id=1, source_target_pairs={{64,0},{128,64},{192,128},{256,192},{320,256},{384,320},{448,384},... | collective-permute-start | bytes 4616 | tf_op jit(solution)/shard_map/while/body/eval_jaxpr/ppermute | solution.py:18
  420.3 7.8 %collective-permute-start.3 = (f32[1,2,4,3,134]{4,2,1,3,0:T(4,128)S(1)}, f32[1,2,4,3,134]{4,2,1,3,0:T(4,128)S(1)}, u32[]{:S(2)}, u32[]{:S(2)}) collective-permute-start(f32[1,2,4,3,134]{4,2,1,3,0:T(4,128)S(1)} %get-tuple-element.280), channel_id=1, source_target_pairs={{0,1},{1,2},{2,3},{3,4},{4,5},{5,6},{6,7},{7,8},{8,9},{9,10},{10,1... | collective-permute-start | bytes 38600 | tf_op jit(solution)/shard_map/while/body/eval_jaxpr/ppermute | solution.py:17
  440.4 8.1 %collective-permute-start.7 = (f32[2,2,4,3,134]{4,2,1,3,0:T(4,128)S(1)}, f32[2,2,4,3,134]{4,2,1,3,0:T(4,128)S(1)}, u32[]{:S(2)}, u32[]{:S(2)}) collective-permute-start(f32[2,2,4,3,134]{4,2,1,3,0:T(4,128)S(1)} %get-tuple-element.286), channel_id=1, source_target_pairs={{0,1},{1,2},{2,3},{3,4},{4,5},{5,6},{6,7},{7,8},{8,9},{9,10},{10,1... | collective-permute-start | bytes 77192 | tf_op jit(solution)/shard_map/while/body/eval_jaxpr/ppermute | solution.py:17
  461.2 8.1 %collective-permute-start.11 = (f32[2,2,4,3,134]{4,2,1,3,0:T(4,128)S(1)}, f32[2,2,4,3,134]{4,2,1,3,0:T(4,128)S(1)}, u32[]{:S(2)}, u32[]{:S(2)}) collective-permute-start(f32[2,2,4,3,134]{4,2,1,3,0:T(4,128)S(1)} %get-tuple-element.290), channel_id=1, source_target_pairs={{0,1},{1,2},{2,3},{3,4},{4,5},{5,6},{6,7},{7,8},{8,9},{9,10},{10,1... | collective-permute-start | bytes 77192 | tf_op jit(solution)/shard_map/while/body/eval_jaxpr/ppermute | solution.py:17
  474.5 8.5 %collective-permute-start = (f32[1,2,4,16,3]{4,2,1,3,0:T(4,128)S(1)}, f32[1,2,4,16,3]{4,2,1,3,0:T(4,128)S(1)}, u32[]{:S(2)}, u32[]{:S(2)}) collective-permute-start(f32[1,2,4,16,3]{4,2,1,3,0:T(4,128)S(1)} %get-tuple-element.277), channel_id=1, source_target_pairs={{64,0},{128,64},{192,128},{256,192},{320,256},{384,320},{448,384},... | collective-permute-start | bytes 4616 | tf_op jit(solution)/shard_map/while/body/eval_jaxpr/ppermute | solution.py:18
  505.2 8.1 %collective-permute-start.7 = (f32[2,2,4,3,134]{4,2,1,3,0:T(4,128)S(1)}, f32[2,2,4,3,134]{4,2,1,3,0:T(4,128)S(1)}, u32[]{:S(2)}, u32[]{:S(2)}) collective-permute-start(f32[2,2,4,3,134]{4,2,1,3,0:T(4,128)S(1)} %get-tuple-element.286), channel_id=1, source_target_pairs={{0,1},{1,2},{2,3},{3,4},{4,5},{5,6},{6,7},{7,8},{8,9},{9,10},{10,1... | collective-permute-start | bytes 77192 | tf_op jit(solution)/shard_map/while/body/eval_jaxpr/ppermute | solution.py:17
  526.0 8.1 %collective-permute-start.11 = (f32[2,2,4,3,134]{4,2,1,3,0:T(4,128)S(1)}, f32[2,2,4,3,134]{4,2,1,3,0:T(4,128)S(1)}, u32[]{:S(2)}, u32[]{:S(2)}) collective-permute-start(f32[2,2,4,3,134]{4,2,1,3,0:T(4,128)S(1)} %get-tuple-element.290), channel_id=1, source_target_pairs={{0,1},{1,2},{2,3},{3,4},{4,5},{5,6},{6,7},{7,8},{8,9},{9,10},{10,1... | collective-permute-start | bytes 77192 | tf_op jit(solution)/shard_map/while/body/eval_jaxpr/ppermute | solution.py:17
  (67 other events, 424.8 us)
where the time goes:
time: 557 us; the launch traced here: 554 us
  starting transfers between devices  312 us (56%)
  waiting for transfers between devices  113 us (20%)
  other arithmetic  86.8 us (16%)
  matrix products  15.4 us (3%)
  blocking collectives  14.2 us (3%)
  local copies, waits for them, and re-layouts  8.81 us (2%)
    ppermute x48, starting transfers between devices, extended(): before = lax.ppermute(last, axis, up)  221 us
    ppermute x48, waiting for transfers between devices, extended(): before = lax.ppermute(last, axis, up)  108 us
    ppermute x48, starting transfers between devices, extended(): after = lax.ppermute(initial, axis, down)  86.8 us
    select_n x72, other arithmetic, clip_domain(): return jnp.where(keep, field, 0.0)  49.1 us
    dot_general x80, matrix products, coefficients(): jnp.einsum('cij,fcp->fpij', onehot, table_part[:, :, :, degree], precisio...  15.4 us
    all_to_all x1, blocking collectives, body(): lax.all_to_all(image, 'depth', split_axis=0, concat_axis=2, tiled=True)  14.2 us
  transfers between devices with their start and end apart: 97, of which 41 were waited for; matrix products, arithmetic and copies ran while one was open for 3% of the time, Pallas kernels for 0%

commit v1 on v0

--- a/solution.py
+++ b/solution.py
@@ -135,7 +135,10 @@
 
     initial = (fields, jnp.zeros((velocity.shape[0], velocity.shape[1], col_count), jnp.float32))
     fields, image = lax.fori_loop(0, velocity.shape[0], descend, initial)
-    return lax.all_to_all(image, "depth", split_axis=0, concat_axis=2, tiled=True)
+    return jnp.concatenate(
+        lax.all_to_all(jnp.stack(jnp.split(image, lax.axis_size("depth"), axis=0)), "depth", 0, 0),
+        axis=2,
+    )
 
 
 def solution(mesh):

time: 557 us -> 557 us (level)
  no operation moved by 1% of the time
where the time goes in v1:
time: 557 us; the launch traced here: 554 us
  starting transfers between devices  312 us (56%)
  waiting for transfers between devices  113 us (20%)
  other arithmetic  86.8 us (16%)
  matrix products  15.4 us (3%)
  blocking collectives  14.2 us (3%)
  local copies, waits for them, and re-layouts  8.83 us (2%)
    ppermute x48, starting transfers between devices, extended(): before = lax.ppermute(last, axis, up)  221 us
    ppermute x48, waiting for transfers between devices, extended(): before = lax.ppermute(last, axis, up)  108 us
    ppermute x48, starting transfers between devices, extended(): after = lax.ppermute(initial, axis, down)  86.8 us
    select_n x72, other arithmetic, clip_domain(): return jnp.where(keep, field, 0.0)  49.1 us
    dot_general x80, matrix products, coefficients(): jnp.einsum('cij,fcp->fpij', onehot, table_part[:, :, :, degree], precisio...  15.4 us
    all_to_all x1, blocking collectives, body(): lax.all_to_all(jnp.stack(jnp.split(image, lax.axis_size('depth'), axis=0)...  14.2 us
  transfers between devices with their start and end apart: 97, of which 41 were waited for; matrix products, arithmetic and copies ran while one was open for 3% of the time, Pallas kernels for 0%

profile of v1, /device:TPU:24, one launch (start us, length us, event | category | flops | bytes accessed | tf_op | source)
XLA Modules:
  0.0 554.2 jit_solution(2505491088299950112)
XLA Ops:
  4.6 4.3 all-to-all-start
  9.7 4.8 all-to-all-done
  16.5 522.7 %while.19 = (s32[]{:T(128)}, f32[2,4,16,128]{3,1,0,2:T(4,128)S(1)}, f32[8,16,128]{2,1,0:T(8,128)S(1)}, s32[8,16,128]{2,0,1:T(8,128)S(1)}, f32[2,8,2,10]{1,2,0,3:...) while((s32[]{:T(128)}, f32[2,4,16,128]{3,1,0,2:T(4,128)S(1)}, ...), condition=%wide.region_1.2_spmd.clone, body=%wide.region_0.1_spmd.clone.sunk | while | flops 12695103 | bytes 9011121 | solution.py:137
  22.6 11.6 %collective-permute-start.2 = (f32[1,2,4,3,134]{4,2,1,3,0:T(4,128)S(1)}, f32[1,2,4,3,134]{4,2,1,3,0:T(4,128)S(1)}, u32[]{:S(2)}, u32[]{:S(2)}) collective-permute-start(f32[1,2,4,3,134]{4,2,1,3,0:T(4,128)S(1)} %get-tuple-element.279), channel_id=1, source_target_pairs={{1,0},{2,1},{3,2},{4,3},{5,4},{6,5},{7,6},{8,7},{9,8},{10,9},{11,1... | collective-permute-start | bytes 38600 | tf_op jit(solution)/shard_map/while/body/eval_jaxpr/ppermute | solution.py:18
  36.2 5.8 %collective-permute-done.3 = f32[1,2,4,3,134]{4,2,1,3,0:T(4,128)S(1)} collective-permute-done((f32[1,2,4,3,134]{4,2,1,3,0:T(4,128)S(1)}, f32[1,2,4,3,134]{4,2,1,3,0:T(4,128)S(1)}, u32[]{:S(2)}, u32[]{:S(2)}) %collective-permute-start.3) | collective-permute-done | bytes 12896 | tf_op jit(solution)/shard_map/while/body/eval_jaxpr/ppermute | solution.py:17
  64.2 5.2 collective-permute-start.9
  87.1 5.9 %collective-permute-start.1 = (f32[1,2,4,16,3]{4,2,1,3,0:T(4,128)S(1)}, f32[1,2,4,16,3]{4,2,1,3,0:T(4,128)S(1)}, u32[]{:S(2)}, u32[]{:S(2)}) collective-permute-start(f32[1,2,4,16,3]{4,2,1,3,0:T(4,128)S(1)} %get-tuple-element.278), channel_id=1, source_target_pairs={{0,64},{64,128},{128,192},{192,256},{256,320},{320,384},{384,448},... | collective-permute-start | bytes 4616 | tf_op jit(solution)/shard_map/while/body/eval_jaxpr/ppermute | solution.py:17
  108.4 5.0 collective-permute-start.5
  128.3 5.9 %collective-permute-start.9 = (f32[2,2,4,16,3]{4,2,1,3,0:T(4,128)S(1)}, f32[2,2,4,16,3]{4,2,1,3,0:T(4,128)S(1)}, u32[]{:S(2)}, u32[]{:S(2)}) collective-permute-start(f32[2,2,4,16,3]{4,2,1,3,0:T(4,128)S(1)} %get-tuple-element.288), channel_id=1, source_target_pairs={{0,64},{64,128},{128,192},{192,256},{256,320},{320,384},{384,448},... | collective-permute-start | bytes 9224 | tf_op jit(solution)/shard_map/while/body/eval_jaxpr/ppermute | solution.py:17
  151.9 5.9 %collective-permute-start.1 = (f32[1,2,4,16,3]{4,2,1,3,0:T(4,128)S(1)}, f32[1,2,4,16,3]{4,2,1,3,0:T(4,128)S(1)}, u32[]{:S(2)}, u32[]{:S(2)}) collective-permute-start(f32[1,2,4,16,3]{4,2,1,3,0:T(4,128)S(1)} %get-tuple-element.278), channel_id=1, source_target_pairs={{0,64},{64,128},{128,192},{192,256},{256,320},{320,384},{384,448},... | collective-permute-start | bytes 4616 | tf_op jit(solution)/shard_map/while/body/eval_jaxpr/ppermute | solution.py:17
  173.2 5.0 collective-permute-start.5
  185.4 4.0 collective-permute-done.7
  193.1 5.9 %collective-permute-start.9 = (f32[2,2,4,16,3]{4,2,1,3,0:T(4,128)S(1)}, f32[2,2,4,16,3]{4,2,1,3,0:T(4,128)S(1)}, u32[]{:S(2)}, u32[]{:S(2)}) collective-permute-start(f32[2,2,4,16,3]{4,2,1,3,0:T(4,128)S(1)} %get-tuple-element.288), channel_id=1, source_target_pairs={{0,64},{64,128},{128,192},{192,256},{256,320},{320,384},{384,448},... | collective-permute-start | bytes 9224 | tf_op jit(solution)/shard_map/while/body/eval_jaxpr/ppermute | solution.py:17
  216.7 5.9 %collective-permute-start.1 = (f32[1,2,4,16,3]{4,2,1,3,0:T(4,128)S(1)}, f32[1,2,4,16,3]{4,2,1,3,0:T(4,128)S(1)}, u32[]{:S(2)}, u32[]{:S(2)}) collective-permute-start(f32[1,2,4,16,3]{4,2,1,3,0:T(4,128)S(1)} %get-tuple-element.278), channel_id=1, source_target_pairs={{0,64},{64,128},{128,192},{192,256},{256,320},{320,384},{384,448},... | collective-permute-start | bytes 4616 | tf_op jit(solution)/shard_map/while/body/eval_jaxpr/ppermute | solution.py:17
  238.0 5.0 collective-permute-start.5
  250.2 4.0 collective-permute-done.7
  257.9 5.9 %collective-permute-start.9 = (f32[2,2,4,16,3]{4,2,1,3,0:T(4,128)S(1)}, f32[2,2,4,16,3]{4,2,1,3,0:T(4,128)S(1)}, u32[]{:S(2)}, u32[]{:S(2)}) collective-permute-start(f32[2,2,4,16,3]{4,2,1,3,0:T(4,128)S(1)} %get-tuple-element.288), channel_id=1, source_target_pairs={{0,64},{64,128},{128,192},{192,256},{256,320},{320,384},{384,448},... | collective-permute-start | bytes 9224 | tf_op jit(solution)/shard_map/while/body/eval_jaxpr/ppermute | solution.py:17
  281.5 5.9 %collective-permute-start.1 = (f32[1,2,4,16,3]{4,2,1,3,0:T(4,128)S(1)}, f32[1,2,4,16,3]{4,2,1,3,0:T(4,128)S(1)}, u32[]{:S(2)}, u32[]{:S(2)}) collective-permute-start(f32[1,2,4,16,3]{4,2,1,3,0:T(4,128)S(1)} %get-tuple-element.278), channel_id=1, source_target_pairs={{0,64},{64,128},{128,192},{192,256},{256,320},{320,384},{384,448},... | collective-permute-start | bytes 4616 | tf_op jit(solution)/shard_map/while/body/eval_jaxpr/ppermute | solution.py:17
  302.8 5.0 collective-permute-start.5
  322.7 5.9 %collective-permute-start.9 = (f32[2,2,4,16,3]{4,2,1,3,0:T(4,128)S(1)}, f32[2,2,4,16,3]{4,2,1,3,0:T(4,128)S(1)}, u32[]{:S(2)}, u32[]{:S(2)}) collective-permute-start(f32[2,2,4,16,3]{4,2,1,3,0:T(4,128)S(1)} %get-tuple-element.288), channel_id=1, source_target_pairs={{0,64},{64,128},{128,192},{192,256},{256,320},{320,384},{384,448},... | collective-permute-start | bytes 9224 | tf_op jit(solution)/shard_map/while/body/eval_jaxpr/ppermute | solution.py:17
  346.3 5.9 %collective-permute-start.1 = (f32[1,2,4,16,3]{4,2,1,3,0:T(4,128)S(1)}, f32[1,2,4,16,3]{4,2,1,3,0:T(4,128)S(1)}, u32[]{:S(2)}, u32[]{:S(2)}) collective-permute-start(f32[1,2,4,16,3]{4,2,1,3,0:T(4,128)S(1)} %get-tuple-element.278), channel_id=1, source_target_pairs={{0,64},{64,128},{128,192},{192,256},{256,320},{320,384},{384,448},... | collective-permute-start | bytes 4616 | tf_op jit(solution)/shard_map/while/body/eval_jaxpr/ppermute | solution.py:17
  367.6 5.0 collective-permute-start.5
  379.8 4.0 collective-permute-done.7
  387.5 5.9 %collective-permute-start.9 = (f32[2,2,4,16,3]{4,2,1,3,0:T(4,128)S(1)}, f32[2,2,4,16,3]{4,2,1,3,0:T(4,128)S(1)}, u32[]{:S(2)}, u32[]{:S(2)}) collective-permute-start(f32[2,2,4,16,3]{4,2,1,3,0:T(4,128)S(1)} %get-tuple-element.288), channel_id=1, source_target_pairs={{0,64},{64,128},{128,192},{192,256},{256,320},{320,384},{384,448},... | collective-permute-start | bytes 9224 | tf_op jit(solution)/shard_map/while/body/eval_jaxpr/ppermute | solution.py:17
  411.0 5.9 %collective-permute-start.1 = (f32[1,2,4,16,3]{4,2,1,3,0:T(4,128)S(1)}, f32[1,2,4,16,3]{4,2,1,3,0:T(4,128)S(1)}, u32[]{:S(2)}, u32[]{:S(2)}) collective-permute-start(f32[1,2,4,16,3]{4,2,1,3,0:T(4,128)S(1)} %get-tuple-element.278), channel_id=1, source_target_pairs={{0,64},{64,128},{128,192},{192,256},{256,320},{320,384},{384,448},... | collective-permute-start | bytes 4616 | tf_op jit(solution)/shard_map/while/body/eval_jaxpr/ppermute | solution.py:17
  432.4 5.0 collective-permute-start.5
  444.6 4.0 collective-permute-done.7
  452.3 5.9 %collective-permute-start.9 = (f32[2,2,4,16,3]{4,2,1,3,0:T(4,128)S(1)}, f32[2,2,4,16,3]{4,2,1,3,0:T(4,128)S(1)}, u32[]{:S(2)}, u32[]{:S(2)}) collective-permute-start(f32[2,2,4,16,3]{4,2,1,3,0:T(4,128)S(1)} %get-tuple-element.288), channel_id=1, source_target_pairs={{0,64},{64,128},{128,192},{192,256},{256,320},{320,384},{384,448},... | collective-permute-start | bytes 9224 | tf_op jit(solution)/shard_map/while/body/eval_jaxpr/ppermute | solution.py:17
  475.8 5.9 %collective-permute-start.1 = (f32[1,2,4,16,3]{4,2,1,3,0:T(4,128)S(1)}, f32[1,2,4,16,3]{4,2,1,3,0:T(4,128)S(1)}, u32[]{:S(2)}, u32[]{:S(2)}) collective-permute-start(f32[1,2,4,16,3]{4,2,1,3,0:T(4,128)S(1)} %get-tuple-element.278), channel_id=1, source_target_pairs={{0,64},{64,128},{128,192},{192,256},{256,320},{320,384},{384,448},... | collective-permute-start | bytes 4616 | tf_op jit(solution)/shard_map/while/body/eval_jaxpr/ppermute | solution.py:17
  497.2 5.0 collective-permute-start.5
  517.1 5.9 %collective-permute-start.9 = (f32[2,2,4,16,3]{4,2,1,3,0:T(4,128)S(1)}, f32[2,2,4,16,3]{4,2,1,3,0:T(4,128)S(1)}, u32[]{:S(2)}, u32[]{:S(2)}) collective-permute-start(f32[2,2,4,16,3]{4,2,1,3,0:T(4,128)S(1)} %get-tuple-element.288), channel_id=1, source_target_pairs={{0,64},{64,128},{128,192},{192,256},{256,320},{320,384},{384,448},... | collective-permute-start | bytes 9224 | tf_op jit(solution)/shard_map/while/body/eval_jaxpr/ppermute | solution.py:17
  539.3 14.2 %all_to_all.23 = f32[8,1,16,128]{3,2,1,0:T(8,128)S(1)} all-to-all(f32[8,1,16,128]{3,2,1,0:T(8,128)S(1)} %constant_dynamic-update-slice_fusion.1), channel_id=1, replica_groups=mesh['depth'=8,'strip'=64] {'depth'}, dimensions={0} | all-to-all | bytes 131072 | tf_op jit(solution)/shard_map/all_to_all | solution.py:139
  (540 shorter events, 370.8 us)
Async XLA Ops:
  4.6 9.9 %all-to-all-start = ((s32[8,1,2048]{2,1,0:T(1,128)}), s32[8,1,2048]{2,1,0:T(1,128)S(1)}, u32[]{:S(2)}, u32[]{:S(2)}) async-start(s32[8,1,2048]{2,1,0:T(1,128)} %reshape.222), calls=%async_computation | async-start | bytes 131072 | tf_op jit(solution)/shard_map/all_to_all | solution.py:124
  22.6 13.6 %collective-permute-start.2 = (f32[1,2,4,3,134]{4,2,1,3,0:T(4,128)S(1)}, f32[1,2,4,3,134]{4,2,1,3,0:T(4,128)S(1)}, u32[]{:S(2)}, u32[]{:S(2)}) collective-permute-start(f32[1,2,4,3,134]{4,2,1,3,0:T(4,128)S(1)} %get-tuple-element.279), channel_id=1, source_target_pairs={{1,0},{2,1},{3,2},{4,3},{5,4},{6,5},{7,6},{8,7},{9,8},{10,9},{11,1... | collective-permute-start | bytes 38600 | tf_op jit(solution)/shard_map/while/body/eval_jaxpr/ppermute | solution.py:18
  34.2 7.8 %collective-permute-start.3 = (f32[1,2,4,3,134]{4,2,1,3,0:T(4,128)S(1)}, f32[1,2,4,3,134]{4,2,1,3,0:T(4,128)S(1)}, u32[]{:S(2)}, u32[]{:S(2)}) collective-permute-start(f32[1,2,4,3,134]{4,2,1,3,0:T(4,128)S(1)} %get-tuple-element.280), channel_id=1, source_target_pairs={{0,1},{1,2},{2,3},{3,4},{4,5},{5,6},{6,7},{7,8},{8,9},{9,10},{10,1... | collective-permute-start | bytes 38600 | tf_op jit(solution)/shard_map/while/body/eval_jaxpr/ppermute | solution.py:17
  52.3 8.1 %collective-permute-start.7 = (f32[2,2,4,3,134]{4,2,1,3,0:T(4,128)S(1)}, f32[2,2,4,3,134]{4,2,1,3,0:T(4,128)S(1)}, u32[]{:S(2)}, u32[]{:S(2)}) collective-permute-start(f32[2,2,4,3,134]{4,2,1,3,0:T(4,128)S(1)} %get-tuple-element.286), channel_id=1, source_target_pairs={{0,1},{1,2},{2,3},{3,4},{4,5},{5,6},{6,7},{7,8},{8,9},{9,10},{10,1... | collective-permute-start | bytes 77192 | tf_op jit(solution)/shard_map/while/body/eval_jaxpr/ppermute | solution.py:17
  72.4 8.1 %collective-permute-start.11 = (f32[2,2,4,3,134]{4,2,1,3,0:T(4,128)S(1)}, f32[2,2,4,3,134]{4,2,1,3,0:T(4,128)S(1)}, u32[]{:S(2)}, u32[]{:S(2)}) collective-permute-start(f32[2,2,4,3,134]{4,2,1,3,0:T(4,128)S(1)} %get-tuple-element.290), channel_id=1, source_target_pairs={{0,1},{1,2},{2,3},{3,4},{4,5},{5,6},{6,7},{7,8},{8,9},{9,10},{10,1... | collective-permute-start | bytes 77192 | tf_op jit(solution)/shard_map/while/body/eval_jaxpr/ppermute | solution.py:17
  85.8 8.5 %collective-permute-start = (f32[1,2,4,16,3]{4,2,1,3,0:T(4,128)S(1)}, f32[1,2,4,16,3]{4,2,1,3,0:T(4,128)S(1)}, u32[]{:S(2)}, u32[]{:S(2)}) collective-permute-start(f32[1,2,4,16,3]{4,2,1,3,0:T(4,128)S(1)} %get-tuple-element.277), channel_id=1, source_target_pairs={{64,0},{128,64},{192,128},{256,192},{320,256},{384,320},{448,384},... | collective-permute-start | bytes 4616 | tf_op jit(solution)/shard_map/while/body/eval_jaxpr/ppermute | solution.py:18
  96.3 7.8 %collective-permute-start.3 = (f32[1,2,4,3,134]{4,2,1,3,0:T(4,128)S(1)}, f32[1,2,4,3,134]{4,2,1,3,0:T(4,128)S(1)}, u32[]{:S(2)}, u32[]{:S(2)}) collective-permute-start(f32[1,2,4,3,134]{4,2,1,3,0:T(4,128)S(1)} %get-tuple-element.280), channel_id=1, source_target_pairs={{0,1},{1,2},{2,3},{3,4},{4,5},{5,6},{6,7},{7,8},{8,9},{9,10},{10,1... | collective-permute-start | bytes 38600 | tf_op jit(solution)/shard_map/while/body/eval_jaxpr/ppermute | solution.py:17
  116.5 8.1 %collective-permute-start.7 = (f32[2,2,4,3,134]{4,2,1,3,0:T(4,128)S(1)}, f32[2,2,4,3,134]{4,2,1,3,0:T(4,128)S(1)}, u32[]{:S(2)}, u32[]{:S(2)}) collective-permute-start(f32[2,2,4,3,134]{4,2,1,3,0:T(4,128)S(1)} %get-tuple-element.286), channel_id=1, source_target_pairs={{0,1},{1,2},{2,3},{3,4},{4,5},{5,6},{6,7},{7,8},{8,9},{9,10},{10,1... | collective-permute-start | bytes 77192 | tf_op jit(solution)/shard_map/while/body/eval_jaxpr/ppermute | solution.py:17
  137.2 8.1 %collective-permute-start.11 = (f32[2,2,4,3,134]{4,2,1,3,0:T(4,128)S(1)}, f32[2,2,4,3,134]{4,2,1,3,0:T(4,128)S(1)}, u32[]{:S(2)}, u32[]{:S(2)}) collective-permute-start(f32[2,2,4,3,134]{4,2,1,3,0:T(4,128)S(1)} %get-tuple-element.290), channel_id=1, source_target_pairs={{0,1},{1,2},{2,3},{3,4},{4,5},{5,6},{6,7},{7,8},{8,9},{9,10},{10,1... | collective-permute-start | bytes 77192 | tf_op jit(solution)/shard_map/while/body/eval_jaxpr/ppermute | solution.py:17
  150.6 8.5 %collective-permute-start = (f32[1,2,4,16,3]{4,2,1,3,0:T(4,128)S(1)}, f32[1,2,4,16,3]{4,2,1,3,0:T(4,128)S(1)}, u32[]{:S(2)}, u32[]{:S(2)}) collective-permute-start(f32[1,2,4,16,3]{4,2,1,3,0:T(4,128)S(1)} %get-tuple-element.277), channel_id=1, source_target_pairs={{64,0},{128,64},{192,128},{256,192},{320,256},{384,320},{448,384},... | collective-permute-start | bytes 4616 | tf_op jit(solution)/shard_map/while/body/eval_jaxpr/ppermute | solution.py:18
  161.1 7.8 %collective-permute-start.3 = (f32[1,2,4,3,134]{4,2,1,3,0:T(4,128)S(1)}, f32[1,2,4,3,134]{4,2,1,3,0:T(4,128)S(1)}, u32[]{:S(2)}, u32[]{:S(2)}) collective-permute-start(f32[1,2,4,3,134]{4,2,1,3,0:T(4,128)S(1)} %get-tuple-element.280), channel_id=1, source_target_pairs={{0,1},{1,2},{2,3},{3,4},{4,5},{5,6},{6,7},{7,8},{8,9},{9,10},{10,1... | collective-permute-start | bytes 38600 | tf_op jit(solution)/shard_map/while/body/eval_jaxpr/ppermute | solution.py:17
  181.3 8.1 %collective-permute-start.7 = (f32[2,2,4,3,134]{4,2,1,3,0:T(4,128)S(1)}, f32[2,2,4,3,134]{4,2,1,3,0:T(4,128)S(1)}, u32[]{:S(2)}, u32[]{:S(2)}) collective-permute-start(f32[2,2,4,3,134]{4,2,1,3,0:T(4,128)S(1)} %get-tuple-element.286), channel_id=1, source_target_pairs={{0,1},{1,2},{2,3},{3,4},{4,5},{5,6},{6,7},{7,8},{8,9},{9,10},{10,1... | collective-permute-start | bytes 77192 | tf_op jit(solution)/shard_map/while/body/eval_jaxpr/ppermute | solution.py:17
  202.0 8.1 %collective-permute-start.11 = (f32[2,2,4,3,134]{4,2,1,3,0:T(4,128)S(1)}, f32[2,2,4,3,134]{4,2,1,3,0:T(4,128)S(1)}, u32[]{:S(2)}, u32[]{:S(2)}) collective-permute-start(f32[2,2,4,3,134]{4,2,1,3,0:T(4,128)S(1)} %get-tuple-element.290), channel_id=1, source_target_pairs={{0,1},{1,2},{2,3},{3,4},{4,5},{5,6},{6,7},{7,8},{8,9},{9,10},{10,1... | collective-permute-start | bytes 77192 | tf_op jit(solution)/shard_map/while/body/eval_jaxpr/ppermute | solution.py:17
  215.4 8.5 %collective-permute-start = (f32[1,2,4,16,3]{4,2,1,3,0:T(4,128)S(1)}, f32[1,2,4,16,3]{4,2,1,3,0:T(4,128)S(1)}, u32[]{:S(2)}, u32[]{:S(2)}) collective-permute-start(f32[1,2,4,16,3]{4,2,1,3,0:T(4,128)S(1)} %get-tuple-element.277), channel_id=1, source_target_pairs={{64,0},{128,64},{192,128},{256,192},{320,256},{384,320},{448,384},... | collective-permute-start | bytes 4616 | tf_op jit(solution)/shard_map/while/body/eval_jaxpr/ppermute | solution.py:18
  225.9 7.8 %collective-permute-start.3 = (f32[1,2,4,3,134]{4,2,1,3,0:T(4,128)S(1)}, f32[1,2,4,3,134]{4,2,1,3,0:T(4,128)S(1)}, u32[]{:S(2)}, u32[]{:S(2)}) collective-permute-start(f32[1,2,4,3,134]{4,2,1,3,0:T(4,128)S(1)} %get-tuple-element.280), channel_id=1, source_target_pairs={{0,1},{1,2},{2,3},{3,4},{4,5},{5,6},{6,7},{7,8},{8,9},{9,10},{10,1... | collective-permute-start | bytes 38600 | tf_op jit(solution)/shard_map/while/body/eval_jaxpr/ppermute | solution.py:17
  246.1 8.1 %collective-permute-start.7 = (f32[2,2,4,3,134]{4,2,1,3,0:T(4,128)S(1)}, f32[2,2,4,3,134]{4,2,1,3,0:T(4,128)S(1)}, u32[]{:S(2)}, u32[]{:S(2)}) collective-permute-start(f32[2,2,4,3,134]{4,2,1,3,0:T(4,128)S(1)} %get-tuple-element.286), channel_id=1, source_target_pairs={{0,1},{1,2},{2,3},{3,4},{4,5},{5,6},{6,7},{7,8},{8,9},{9,10},{10,1... | collective-permute-start | bytes 77192 | tf_op jit(solution)/shard_map/while/body/eval_jaxpr/ppermute | solution.py:17
  266.8 8.1 %collective-permute-start.11 = (f32[2,2,4,3,134]{4,2,1,3,0:T(4,128)S(1)}, f32[2,2,4,3,134]{4,2,1,3,0:T(4,128)S(1)}, u32[]{:S(2)}, u32[]{:S(2)}) collective-permute-start(f32[2,2,4,3,134]{4,2,1,3,0:T(4,128)S(1)} %get-tuple-element.290), channel_id=1, source_target_pairs={{0,1},{1,2},{2,3},{3,4},{4,5},{5,6},{6,7},{7,8},{8,9},{9,10},{10,1... | collective-permute-start | bytes 77192 | tf_op jit(solution)/shard_map/while/body/eval_jaxpr/ppermute | solution.py:17
  280.2 8.5 %collective-permute-start = (f32[1,2,4,16,3]{4,2,1,3,0:T(4,128)S(1)}, f32[1,2,4,16,3]{4,2,1,3,0:T(4,128)S(1)}, u32[]{:S(2)}, u32[]{:S(2)}) collective-permute-start(f32[1,2,4,16,3]{4,2,1,3,0:T(4,128)S(1)} %get-tuple-element.277), channel_id=1, source_target_pairs={{64,0},{128,64},{192,128},{256,192},{320,256},{384,320},{448,384},... | collective-permute-start | bytes 4616 | tf_op jit(solution)/shard_map/while/body/eval_jaxpr/ppermute | solution.py:18
  290.7 7.8 %collective-permute-start.3 = (f32[1,2,4,3,134]{4,2,1,3,0:T(4,128)S(1)}, f32[1,2,4,3,134]{4,2,1,3,0:T(4,128)S(1)}, u32[]{:S(2)}, u32[]{:S(2)}) collective-permute-start(f32[1,2,4,3,134]{4,2,1,3,0:T(4,128)S(1)} %get-tuple-element.280), channel_id=1, source_target_pairs={{0,1},{1,2},{2,3},{3,4},{4,5},{5,6},{6,7},{7,8},{8,9},{9,10},{10,1... | collective-permute-start | bytes 38600 | tf_op jit(solution)/shard_map/while/body/eval_jaxpr/ppermute | solution.py:17
  310.9 8.1 %collective-permute-start.7 = (f32[2,2,4,3,134]{4,2,1,3,0:T(4,128)S(1)}, f32[2,2,4,3,134]{4,2,1,3,0:T(4,128)S(1)}, u32[]{:S(2)}, u32[]{:S(2)}) collective-permute-start(f32[2,2,4,3,134]{4,2,1,3,0:T(4,128)S(1)} %get-tuple-element.286), channel_id=1, source_target_pairs={{0,1},{1,2},{2,3},{3,4},{4,5},{5,6},{6,7},{7,8},{8,9},{9,10},{10,1... | collective-permute-start | bytes 77192 | tf_op jit(solution)/shard_map/while/body/eval_jaxpr/ppermute | solution.py:17
  331.6 8.1 %collective-permute-start.11 = (f32[2,2,4,3,134]{4,2,1,3,0:T(4,128)S(1)}, f32[2,2,4,3,134]{4,2,1,3,0:T(4,128)S(1)}, u32[]{:S(2)}, u32[]{:S(2)}) collective-permute-start(f32[2,2,4,3,134]{4,2,1,3,0:T(4,128)S(1)} %get-tuple-element.290), channel_id=1, source_target_pairs={{0,1},{1,2},{2,3},{3,4},{4,5},{5,6},{6,7},{7,8},{8,9},{9,10},{10,1... | collective-permute-start | bytes 77192 | tf_op jit(solution)/shard_map/while/body/eval_jaxpr/ppermute | solution.py:17
  345.0 8.5 %collective-permute-start = (f32[1,2,4,16,3]{4,2,1,3,0:T(4,128)S(1)}, f32[1,2,4,16,3]{4,2,1,3,0:T(4,128)S(1)}, u32[]{:S(2)}, u32[]{:S(2)}) collective-permute-start(f32[1,2,4,16,3]{4,2,1,3,0:T(4,128)S(1)} %get-tuple-element.277), channel_id=1, source_target_pairs={{64,0},{128,64},{192,128},{256,192},{320,256},{384,320},{448,384},... | collective-permute-start | bytes 4616 | tf_op jit(solution)/shard_map/while/body/eval_jaxpr/ppermute | solution.py:18
  355.5 7.8 %collective-permute-start.3 = (f32[1,2,4,3,134]{4,2,1,3,0:T(4,128)S(1)}, f32[1,2,4,3,134]{4,2,1,3,0:T(4,128)S(1)}, u32[]{:S(2)}, u32[]{:S(2)}) collective-permute-start(f32[1,2,4,3,134]{4,2,1,3,0:T(4,128)S(1)} %get-tuple-element.280), channel_id=1, source_target_pairs={{0,1},{1,2},{2,3},{3,4},{4,5},{5,6},{6,7},{7,8},{8,9},{9,10},{10,1... | collective-permute-start | bytes 38600 | tf_op jit(solution)/shard_map/while/body/eval_jaxpr/ppermute | solution.py:17
  375.6 8.1 %collective-permute-start.7 = (f32[2,2,4,3,134]{4,2,1,3,0:T(4,128)S(1)}, f32[2,2,4,3,134]{4,2,1,3,0:T(4,128)S(1)}, u32[]{:S(2)}, u32[]{:S(2)}) collective-permute-start(f32[2,2,4,3,134]{4,2,1,3,0:T(4,128)S(1)} %get-tuple-element.286), channel_id=1, source_target_pairs={{0,1},{1,2},{2,3},{3,4},{4,5},{5,6},{6,7},{7,8},{8,9},{9,10},{10,1... | collective-permute-start | bytes 77192 | tf_op jit(solution)/shard_map/while/body/eval_jaxpr/ppermute | solution.py:17
  396.4 8.1 %collective-permute-start.11 = (f32[2,2,4,3,134]{4,2,1,3,0:T(4,128)S(1)}, f32[2,2,4,3,134]{4,2,1,3,0:T(4,128)S(1)}, u32[]{:S(2)}, u32[]{:S(2)}) collective-permute-start(f32[2,2,4,3,134]{4,2,1,3,0:T(4,128)S(1)} %get-tuple-element.290), channel_id=1, source_target_pairs={{0,1},{1,2},{2,3},{3,4},{4,5},{5,6},{6,7},{7,8},{8,9},{9,10},{10,1... | collective-permute-start | bytes 77192 | tf_op jit(solution)/shard_map/while/body/eval_jaxpr/ppermute | solution.py:17
  409.7 8.5 %collective-permute-start = (f32[1,2,4,16,3]{4,2,1,3,0:T(4,128)S(1)}, f32[1,2,4,16,3]{4,2,1,3,0:T(4,128)S(1)}, u32[]{:S(2)}, u32[]{:S(2)}) collective-permute-start(f32[1,2,4,16,3]{4,2,1,3,0:T(4,128)S(1)} %get-tuple-element.277), channel_id=1, source_target_pairs={{64,0},{128,64},{192,128},{256,192},{320,256},{384,320},{448,384},... | collective-permute-start | bytes 4616 | tf_op jit(solution)/shard_map/while/body/eval_jaxpr/ppermute | solution.py:18
  420.3 7.8 %collective-permute-start.3 = (f32[1,2,4,3,134]{4,2,1,3,0:T(4,128)S(1)}, f32[1,2,4,3,134]{4,2,1,3,0:T(4,128)S(1)}, u32[]{:S(2)}, u32[]{:S(2)}) collective-permute-start(f32[1,2,4,3,134]{4,2,1,3,0:T(4,128)S(1)} %get-tuple-element.280), channel_id=1, source_target_pairs={{0,1},{1,2},{2,3},{3,4},{4,5},{5,6},{6,7},{7,8},{8,9},{9,10},{10,1... | collective-permute-start | bytes 38600 | tf_op jit(solution)/shard_map/while/body/eval_jaxpr/ppermute | solution.py:17
  440.4 8.1 %collective-permute-start.7 = (f32[2,2,4,3,134]{4,2,1,3,0:T(4,128)S(1)}, f32[2,2,4,3,134]{4,2,1,3,0:T(4,128)S(1)}, u32[]{:S(2)}, u32[]{:S(2)}) collective-permute-start(f32[2,2,4,3,134]{4,2,1,3,0:T(4,128)S(1)} %get-tuple-element.286), channel_id=1, source_target_pairs={{0,1},{1,2},{2,3},{3,4},{4,5},{5,6},{6,7},{7,8},{8,9},{9,10},{10,1... | collective-permute-start | bytes 77192 | tf_op jit(solution)/shard_map/while/body/eval_jaxpr/ppermute | solution.py:17
  461.2 8.1 %collective-permute-start.11 = (f32[2,2,4,3,134]{4,2,1,3,0:T(4,128)S(1)}, f32[2,2,4,3,134]{4,2,1,3,0:T(4,128)S(1)}, u32[]{:S(2)}, u32[]{:S(2)}) collective-permute-start(f32[2,2,4,3,134]{4,2,1,3,0:T(4,128)S(1)} %get-tuple-element.290), channel_id=1, source_target_pairs={{0,1},{1,2},{2,3},{3,4},{4,5},{5,6},{6,7},{7,8},{8,9},{9,10},{10,1... | collective-permute-start | bytes 77192 | tf_op jit(solution)/shard_map/while/body/eval_jaxpr/ppermute | solution.py:17
  474.5 8.5 %collective-permute-start = (f32[1,2,4,16,3]{4,2,1,3,0:T(4,128)S(1)}, f32[1,2,4,16,3]{4,2,1,3,0:T(4,128)S(1)}, u32[]{:S(2)}, u32[]{:S(2)}) collective-permute-start(f32[1,2,4,16,3]{4,2,1,3,0:T(4,128)S(1)} %get-tuple-element.277), channel_id=1, source_target_pairs={{64,0},{128,64},{192,128},{256,192},{320,256},{384,320},{448,384},... | collective-permute-start | bytes 4616 | tf_op jit(solution)/shard_map/while/body/eval_jaxpr/ppermute | solution.py:18
  505.2 8.1 %collective-permute-start.7 = (f32[2,2,4,3,134]{4,2,1,3,0:T(4,128)S(1)}, f32[2,2,4,3,134]{4,2,1,3,0:T(4,128)S(1)}, u32[]{:S(2)}, u32[]{:S(2)}) collective-permute-start(f32[2,2,4,3,134]{4,2,1,3,0:T(4,128)S(1)} %get-tuple-element.286), channel_id=1, source_target_pairs={{0,1},{1,2},{2,3},{3,4},{4,5},{5,6},{6,7},{7,8},{8,9},{9,10},{10,1... | collective-permute-start | bytes 77192 | tf_op jit(solution)/shard_map/while/body/eval_jaxpr/ppermute | solution.py:17
  526.0 8.1 %collective-permute-start.11 = (f32[2,2,4,3,134]{4,2,1,3,0:T(4,128)S(1)}, f32[2,2,4,3,134]{4,2,1,3,0:T(4,128)S(1)}, u32[]{:S(2)}, u32[]{:S(2)}) collective-permute-start(f32[2,2,4,3,134]{4,2,1,3,0:T(4,128)S(1)} %get-tuple-element.290), channel_id=1, source_target_pairs={{0,1},{1,2},{2,3},{3,4},{4,5},{5,6},{6,7},{7,8},{8,9},{9,10},{10,1... | collective-permute-start | bytes 77192 | tf_op jit(solution)/shard_map/while/body/eval_jaxpr/ppermute | solution.py:17
  (67 other events, 424.8 us)
